TPU v7x, 512 devices: a whole 4x8x8 slice. The times are simulated.
512 devices in a mesh: dp: 4 (over z_lo, core), seq: 8 (over y), vocab: 16 (over z_hi, x).
Axes of the slice: x: 4, y: 8, z: 8 (z_hi: 4, z_lo: 2; z = z_hi * 2 + z_lo), core: 2. Of those that a mesh axis runs over, the one named last changes fastest.
Arguments:
- queries: bfloat16 [4, 256, 4096], P('dp', 'seq', 'vocab'), may hold values from -64 to 64
- enc_keys: bfloat16 [4, 1024, 4096], P('dp', 'seq', 'vocab'), may hold values from -6 to 6
- enc_values: bfloat16 [4, 1024, 4096], P('dp', 'seq', 'vocab'), may hold values from -6 to 6
- enc_lengths: int32 [4], P('dp'), may hold values from 256 to 1024, as said below
- out_proj: bfloat16 [4096, 4096], P('vocab', 'seq'), may hold values from -0.375 to 0.375
- residual: bfloat16 [4, 256, 4096], P('dp', None, 'seq'), may hold values from -270 to 270
- norm_gain: float32 [4096], P('seq'), may hold values from 0.4 to 1.6
- head_weight: bfloat16 [4096, 32128], P('seq', 'vocab'), may hold values from -1 to 1
- targets: int32 [4, 256], P('dp', 'seq'), may hold values from 0 to 32127
Outputs:
- mean_loss: float32 [], replicated
- head_grad: bfloat16 [4096, 32128], P('seq', 'vocab')
- key_grad: float32 [4, 1024, 4096], P('dp', 'seq', 'vocab')
- value_grad: float32 [4, 1024, 4096], P('dp', 'seq', 'vocab')
Inputs may be any that keep to these rules, and one draw needn't show every extreme that they name: `enc_lengths`: each example has at least 256 unpadded positions; some example has none padded.
All inputs are finite; a program needn't handle non-finite values.
Results may differ from a plain program's by a relative error of at most 0.02.
Values may be sent and summed in bfloat16 or wider, within the bound.
A program may use at most 64 MiB of HBM per device.

v0:
```python
import jax
import jax.numpy as jnp
from jax import lax
from jax.sharding import PartitionSpec as P

D = 4096
HDIM = 256
zloss_weight = 0.0001
norm_epsilon = 1e-06


def body(
    queries, enc_keys, enc_values, enc_lengths, out_proj, residual, norm_gain, head_weight, targets
):
    examples, tgt_rows, features = queries.shape
    heads_here = features // HDIM
    vocab_cols = head_weight.shape[1]
    all_targets = tgt_rows * lax.axis_size("seq")
    score_scale = HDIM ** (-0.5)
    key_all, value_all = (
        lax.all_gather(enc_keys, "seq", axis=1, tiled=True),
        lax.all_gather(enc_values, "seq", axis=1, tiled=True),
    )
    enc_rows = key_all.shape[1]
    query_heads = queries.reshape(examples, tgt_rows, heads_here, HDIM)
    key_heads = key_all.reshape(examples, enc_rows, heads_here, HDIM)
    value_heads = value_all.reshape(examples, enc_rows, heads_here, HDIM)
    scores = (
        jnp.einsum("bthd,bjhd->bhtj", query_heads, key_heads, preferred_element_type=jnp.float32)
        * score_scale
    )
    valid_keys = lax.broadcasted_iota(jnp.int32, (examples, enc_rows), 1) < enc_lengths[:, None]
    scores = jnp.where(valid_keys[:, None, None, :], scores, -jnp.inf)
    score_peak = jnp.max(scores, axis=-1, keepdims=True)
    score_exp = jnp.exp(scores - score_peak)
    weights_full = score_exp / jnp.sum(score_exp, axis=-1, keepdims=True)
    weights_half = weights_full.astype(jnp.bfloat16)
    attended = jnp.einsum(
        "bhtj,bjhd->tbhd", weights_half, value_heads, preferred_element_type=jnp.float32
    )
    attended = attended.astype(jnp.bfloat16).reshape(tgt_rows, examples, features)
    attended_all = lax.all_gather(attended, "seq", axis=0, tiled=True)
    mixed_part = jnp.einsum(
        "tbf,fd->tbd", attended_all, out_proj, preferred_element_type=jnp.float32
    )
    mixed_rows = lax.psum(mixed_part, "vocab") + jnp.swapaxes(residual, 0, 1).astype(jnp.float32)
    square_sum = lax.psum(jnp.sum(mixed_rows * mixed_rows, axis=-1), "seq")
    inverse_rms = lax.rsqrt(square_sum / D + norm_epsilon)
    normed = (mixed_rows * inverse_rms[..., None] * norm_gain).astype(jnp.bfloat16)
    row_block = normed
    logits = lax.psum_scatter(
        jnp.einsum("tbd,dv->tbv", row_block, head_weight, preferred_element_type=jnp.float32),
        "seq",
        scatter_dimension=0,
        tiled=True,
    )
    column_ids = (
        lax.broadcasted_iota(jnp.int32, (1, 1, vocab_cols), 2)
        + lax.axis_index("vocab") * vocab_cols
    )
    target_hit = column_ids == jnp.swapaxes(targets, 0, 1)[..., None]
    local_target = jnp.sum(jnp.where(target_hit, logits, 0.0), axis=-1)
    row_peak = lax.pmax(jnp.max(logits, axis=-1), "vocab")
    exp_total, target_logit = lax.psum(
        (jnp.sum(jnp.exp(logits - row_peak[..., None]), axis=-1), local_target), "vocab"
    )
    log_total = row_peak + jnp.log(exp_total)
    token_loss = log_total - target_logit + zloss_weight * log_total * log_total
    mean_loss = lax.psum(jnp.sum(token_loss), ("dp", "seq")) / (
        examples * lax.axis_size("dp") * all_targets
    )
    logit_grad = (
        jnp.exp(logits - log_total[..., None]) * (1.0 + 2.0 * zloss_weight * log_total)[..., None]
        - target_hit.astype(jnp.float32)
    ).astype(jnp.bfloat16)
    grad_piece = lax.all_gather(logit_grad, "seq", axis=0, tiled=True)
    row_block = normed
    weight_acc = jnp.einsum(
        "tbd,tbv->dv", row_block, grad_piece, preferred_element_type=jnp.float32
    )
    hidden_part = jnp.einsum(
        "tbv,dv->tbd", grad_piece, head_weight, preferred_element_type=jnp.float32
    )
    head_total = lax.psum(weight_acc.astype(jnp.bfloat16), "dp")
    summed_grad = lax.psum(hidden_part, "vocab")
    gated = summed_grad * norm_gain
    dot_row = lax.psum(jnp.sum(gated * mixed_rows, axis=-1), "seq")
    mixed_grad = (
        gated * inverse_rms[..., None] - mixed_rows * (inverse_rms**3 * dot_row / D)[..., None]
    ).astype(jnp.bfloat16)
    row_block = mixed_grad
    attended_grad = lax.psum_scatter(
        jnp.einsum("tbd,fd->tbf", row_block, out_proj, preferred_element_type=jnp.float32),
        "seq",
        scatter_dimension=0,
        tiled=True,
    ).astype(jnp.bfloat16)
    grad_heads = attended_grad.reshape(tgt_rows, examples, heads_here, HDIM)
    prob_grad = jnp.einsum(
        "tbhd,bjhd->bhtj", grad_heads, value_heads, preferred_element_type=jnp.float32
    )
    score_grad = weights_full * (
        prob_grad - jnp.sum(weights_full * prob_grad, axis=-1, keepdims=True)
    )
    score_half = (score_grad * score_scale).astype(jnp.bfloat16)
    value_part = jnp.einsum(
        "bhtj,tbhd->bjhd", weights_half, grad_heads, preferred_element_type=jnp.float32
    )
    key_part = jnp.einsum(
        "bhtj,bthd->bjhd", score_half, query_heads, preferred_element_type=jnp.float32
    )
    key_grad, value_grad = (
        lax.psum_scatter(
            key_part.reshape(examples, enc_rows, features).astype(jnp.bfloat16),
            "seq",
            scatter_dimension=1,
            tiled=True,
        ).astype(jnp.float32),
        lax.psum_scatter(
            value_part.reshape(examples, enc_rows, features).astype(jnp.bfloat16),
            "seq",
            scatter_dimension=1,
            tiled=True,
        ).astype(jnp.float32),
    )
    return (mean_loss, head_total, key_grad, value_grad)


def solution(mesh):
    placed = (
        P("dp", "seq", "vocab"),
        P("dp", "seq", "vocab"),
        P("dp", "seq", "vocab"),
        P("dp"),
        P("vocab", "seq"),
        P("dp", None, "seq"),
        P("seq"),
        P("seq", "vocab"),
        P("dp", "seq"),
    )
    return jax.shard_map(
        body,
        mesh=mesh,
        in_specs=placed,
        out_specs=(P(), P("seq", "vocab"), P("dp", "seq", "vocab"), P("dp", "seq", "vocab")),
        check_vma=False,
    )
```

profile of v0, /device:TPU:1, one launch (start us, length us, event | category | flops | bytes accessed | tf_op | source)
XLA Modules:
  0.0 880.7 jit_solution(10574764354764928775)
XLA Ops:
  7.2 0.0 copy-start
  7.2 0.0 copy-start.5
  7.2 0.0 all-reduce.7.cloned.1.call-start
  7.2 22.1 %all_gather.12 = bf16[1,1024,256]{2,1,0:T(8,128)(2,1)S(1)} all-gather(bf16[1,128,256]{2,1,0:T(8,128)(2,1)} %param.10), channel_id=1, replica_groups=mesh['dp'=4,'seq'=8,'vocab'=16] {'seq'}, dimensions={1}, use_global_device_ids=true | all-gather | bytes 589824 | tf_op jit(solution)/shard_map/all_gather | solution.py:21
  30.0 19.8 %all_gather.13 = bf16[1,1024,256]{2,1,0:T(8,128)(2,1)S(1)} all-gather(bf16[1,128,256]{2,1,0:T(8,128)(2,1)} %param.11), channel_id=1, replica_groups=mesh['dp'=4,'seq'=8,'vocab'=16] {'seq'}, dimensions={1}, use_global_device_ids=true | all-gather | bytes 589824 | tf_op jit(solution)/shard_map/all_gather | solution.py:22
  49.8 1.1 fusion.42
  51.0 0.2 fusion.21
  51.2 0.0 copy-done.6
  51.2 0.2 fusion.3
  51.5 18.9 %all-gather = bf16[256,1,1,256]{3,0,2,1:T(8,128)(2,1)S(1)} all-gather(bf16[32,1,1,256]{3,0,2,1:T(8,128)(2,1)S(1)} %fusion.3), channel_id=2, replica_groups=mesh['dp'=4,'seq'=8,'vocab'=16] {'seq'}, dimensions={0}, use_global_device_ids=true | all-gather | bytes 147456 | tf_op jit(solution)/shard_map/all_gather | solution.py:42
  70.4 1.0 convolution_bitcast_fusion.2
  71.4 0.0 all-reduce.7.cloned.1.call-update
  71.4 0.0 all-reduce.13.cloned.1.call-start
  71.5 182.3 %all-reduce.7.cloned.1.call-done = f32[256,1,512]{2,0,1:T(8,128)} async-done(((f32[256,1,512]{2,0,1:T(8,128)}), f32[256,1,512]{2,0,1:T(8,128)}) %all-reduce.7.cloned.1.call-update) | async-done | bytes 524304 | tf_op jit(solution)/shard_map/psum | solution.py:46
  253.8 1.2 multiply_reduce_fusion.1
  255.0 13.7 %psum.57 = f32[256,1]{0,1:T(1,128)S(1)} all-reduce(f32[256,1]{0,1:T(1,128)S(1)} %bitcast.113), channel_id=1, replica_groups=mesh['dp'=4,'seq'=8,'vocab'=16] {'seq'}, use_global_device_ids=true, to_apply=%region_4.5 | all-reduce | flops 256 | bytes 2048 | tf_op jit(solution)/shard_map/psum | solution.py:47
  268.7 0.0 copy-done.9
  268.7 1.2 fusion.13
  269.9 2.0 convolution_bitcast_fusion
  271.9 6.1 copy.18
  278.0 0.0 all-reduce.13.cloned.1.call-update
  278.1 0.0 all-reduce.11.cloned.1.call-start
  278.1 1.3 dynamic-slice
  280.1 92.1 %all-reduce.13.cloned.1.call-done = f32[256,1,2008]{2,1,0:T(1,128)} async-done(((f32[256,1,2008]{2,1,0:T(1,128)}), f32[256,1,2008]{2,1,0:T(1,128)}) %all-reduce.13.cloned.1.call-update) | async-done | bytes 2056208
  372.2 1.3 fusion.41
  373.6 38.9 %pmax.7 = f32[32,1]{0,1:T(1,128)S(1)} all-reduce(f32[32,1]{0,1:T(1,128)S(1)} %bitcast.120), channel_id=1, replica_groups=mesh['dp'=4,'seq'=8,'vocab'=16] {'vocab'}, use_global_device_ids=true, to_apply=%region_7.8 | all-reduce | flops 32 | bytes 256 | tf_op jit(solution)/shard_map/pmax | solution.py:63
  412.5 0.6 exponential_reduce_fusion
  413.0 0.2 fusion.10
  413.2 32.1 %all-reduce.1 = (f32[32,1]{0,1:T(1,128)S(1)}, f32[32,1]{0,1:T(1,128)S(1)}) all-reduce(f32[32,1]{0,1:T(1,128)S(1)} %bitcast.118, f32[32,1]{0,1:T(1,128)S(1)} %bitcast.119), channel_id=1, replica_groups=mesh['dp'=4,'seq'=8,'vocab'=16] {'vocab'}, use_global_device_ids=true, to_apply=%region_9.10 | all-reduce | flops 64 | bytes 512 | tf_op jit(solution)/shard_map/psum | solution.py:64
  445.3 0.6 fusion.37
  446.0 0.2 fusion.12
  446.1 20.6 %all_gather.15 = bf16[256,1,2008]{2,0,1:T(8,128)(2,1)S(1)} all-gather(bf16[32,1,2008]{2,0,1:T(8,128)(2,1)S(1)} %fusion.12), channel_id=1, replica_groups=mesh['dp'=4,'seq'=8,'vocab'=16] {'seq'}, dimensions={0}, use_global_device_ids=true | all-gather | bytes 1156608 | tf_op jit(solution)/shard_map/all_gather | solution.py:76
  466.7 1.0 copy-done.2
  467.7 1.5 convolution_bitcast_fusion.1
  469.2 0.0 all-reduce.11.cloned.1.call-update
  469.3 0.0 reduce-scatter.6.cloned.1.call-start
  469.3 178.2 %all-reduce.11.cloned.1.call-done = f32[256,1,512]{2,0,1:T(8,128)} async-done(((f32[256,1,512]{2,0,1:T(8,128)}), f32[256,1,512]{2,0,1:T(8,128)}) %all-reduce.11.cloned.1.call-update) | async-done | bytes 524304 | tf_op jit(solution)/shard_map/psum | solution.py:85
  647.5 1.2 multiply_reduce_fusion
  648.8 13.7 %psum.63 = f32[256,1]{0,1:T(1,128)S(1)} all-reduce(f32[256,1]{0,1:T(1,128)S(1)} %bitcast.114), channel_id=1, replica_groups=mesh['dp'=4,'seq'=8,'vocab'=16] {'seq'}, use_global_device_ids=true, to_apply=%region_17.18 | all-reduce | flops 256 | bytes 2048 | tf_op jit(solution)/shard_map/psum | solution.py:87
  662.5 2.1 convolution_bitcast_fusion.3
  664.5 0.0 reduce-scatter.6.cloned.1.call-update
  664.5 0.0 reduce-scatter.10.cloned.1.call-start
  664.6 43.5 %reduce-scatter.6.cloned.1.call-done = f32[32,1,256]{2,0,1:T(8,128)} async-done(((f32[256,1,256]{2,0,1:T(8,128)}), f32[32,1,256]{2,0,1:T(8,128)}) %reduce-scatter.6.cloned.1.call-update) | async-done | bytes 32784 | tf_op jit(solution)/shard_map/reduce_scatter | solution.py:92
  708.1 1.2 fusion.1
  709.3 0.0 copy-start.7
  709.3 2.0 copy.22
  711.3 2.2 copy.28
  713.5 0.0 reduce-scatter.10.cloned.1.call-update
  713.5 0.0 reduce-scatter.8.cloned.1.call-start
  713.6 1.4 multiply_reduce_fusion.2
  715.0 1.2 fusion
  716.2 0.0 reduce-scatter.8.cloned.1.call-update
  716.2 0.0 all-reduce.9.cloned.1.call-start
  716.3 2.0 convolution_convert_fusion
  718.4 0.0 all-reduce.9.cloned.1.call-update
  718.4 60.4 %psum.60 = f32[]{:T(128)} all-reduce(f32[]{:T(128)} %get-tuple-element.26), channel_id=1, replica_groups=mesh['dp'=4,'seq'=8,'vocab'=16] {'dp','seq'}, use_global_device_ids=true, to_apply=%region_13.14 | all-reduce | flops 1 | bytes 8 | tf_op jit(solution)/shard_map/psum | solution.py:69
  779.4 0.0 reduce-scatter.10.cloned.1.call-done
  779.4 0.9 reshape_bitcast_fusion
  780.4 0.1 copy.23
  780.5 0.8 copy.21
  781.3 13.0 %reduce-scatter.8.cloned.1.call-done = bf16[1,128,256]{2,1,0:T(8,128)(2,1)} async-done(((bf16[1,1024,256]{2,1,0:T(8,128)(2,1)}), bf16[1,128,256]{2,1,0:T(8,128)(2,1)}) %reduce-scatter.8.cloned.1.call-update) | async-done | bytes 65552 | tf_op jit(solution)/shard_map/reduce_scatter | solution.py:113
  794.3 1.5 convert_element_type.128
  795.8 74.0 %all-reduce.9.cloned.1.call-done = bf16[512,2008]{0,1:T(8,128)(2,1)} async-done(((bf16[512,2008]{0,1:T(8,128)(2,1)}), bf16[512,2008]{0,1:T(8,128)(2,1)}) %all-reduce.9.cloned.1.call-update) | async-done | bytes 2056208 | tf_op jit(solution)/shard_map/psum | solution.py:84
  869.7 3.0 copy.34
  (20 shorter events, 0.1 us)
Async XLA Ops:
  7.2 262.7 %copy-start = (bf16[512,2008]{0,1:T(8,128)(2,1)S(1)}, bf16[512,2008]{0,1:T(8,128)(2,1)}, u32[]{:S(2)}) copy-start(bf16[512,2008]{0,1:T(8,128)(2,1)} %param.16) | copy-start | bytes 6168580
  7.2 63.2 %copy-start.5 = (bf16[256,512]{1,0:T(8,128)(2,1)S(1)}, bf16[256,512]{1,0:T(8,128)(2,1)}, u32[]{:S(2)}) copy-start(bf16[256,512]{1,0:T(8,128)(2,1)} %param.13) | copy-start | bytes 786436
  7.2 246.6 %all-reduce.7.cloned.1.call-start = ((), (), s32[]{:S(2)}) async-start(), calls=%async_computation.3 | async-start | bytes 1048576 | tf_op jit(solution)/shard_map/psum | solution.py:46
  29.3 224.5 %copy-start.4 = (bf16[1,256,512]{2,1,0:T(8,128)(2,1)S(1)}, bf16[1,256,512]{2,1,0:T(8,128)(2,1)}, u32[]{:S(2)}) copy-start(bf16[1,256,512]{2,1,0:T(8,128)(2,1)} %param.14) | copy-start | bytes 786436
  49.8 1.4 copy-start.6
  49.8 218.9 %copy-start.9 = (f32[512]{0:T(512)S(1)}, f32[512]{0:T(512)}, u32[]{:S(2)}) copy-start(f32[512]{0:T(512)} %param.15) | copy-start | bytes 6148
  71.4 300.8 %all-reduce.13.cloned.1.call-start = ((), (), s32[]{:S(2)}) async-start(), calls=%async_computation.9 | async-start | bytes 4194304
  278.0 135.0 %copy-start.10 = (s32[1,32]{1,0:T(1,128)S(1)}, s32[1,32]{1,0:T(1,128)}, u32[]{:S(2)}) copy-start(s32[1,32]{1,0:T(1,128)} %param.17) | copy-start | bytes 388
  278.1 369.5 %all-reduce.11.cloned.1.call-start = ((), (), s32[]{:S(2)}) async-start(), calls=%async_computation.5 | async-start | bytes 1048576 | tf_op jit(solution)/shard_map/psum | solution.py:85
  466.7 1.0 copy-start.2
  467.7 179.8 %copy-start.1 = (f32[256,1,512]{2,0,1:T(8,128)S(1)}, f32[256,1,512]{2,0,1:T(8,128)}, u32[]{:S(2)}) copy-start(f32[256,1,512]{2,0,1:T(8,128)} %all-reduce.7.cloned.1.call-done) | copy-start | bytes 1572868
  469.3 238.8 %reduce-scatter.6.cloned.1.call-start = ((), (), s32[]{:S(2)}) async-start(), calls=%async_computation.6 | async-start | bytes 294912 | tf_op jit(solution)/shard_map/reduce_scatter | solution.py:92
  664.5 114.9 %reduce-scatter.10.cloned.1.call-start = ((), (), s32[]{:S(2)}) async-start(), calls=%async_computation.8 | async-start | bytes 589824
  708.1 5.5 copy-start.8
  709.3 5.7 copy-start.7
  711.3 5.0 copy-start.3
  713.5 80.8 %reduce-scatter.8.cloned.1.call-start = ((), (), s32[]{:S(2)}) async-start(), calls=%async_computation.7 | async-start | bytes 589824 | tf_op jit(solution)/shard_map/reduce_scatter | solution.py:113
  716.2 153.5 %all-reduce.9.cloned.1.call-start = ((), (), s32[]{:S(2)}) async-start(), calls=%async_computation.4 | async-start | bytes 4112384 | tf_op jit(solution)/shard_map/psum | solution.py:84
Sparse Core Ops, SparseCore 0:
  71.6 182.1 all-reduce.6
  278.2 93.9 all-reduce.12
  469.4 178.1 all-reduce.10
  664.7 43.3 reduce-scatter.5
  713.6 39.4 reduce-scatter.9
  755.8 38.4 reduce-scatter.7
  798.1 71.5 all-reduce.8
where the time goes:
time: 882 us; the launch traced here: 881 us
  waiting for transfers between devices  583 us (66%)
  blocking collectives  240 us (27%)
  local copies, waits for them, and re-layouts  17.4 us (2%)
  between operations  17.4 us (2%)
  matrix products  13.9 us (2%)
    psum x1, waiting for transfers between devices, body(): lax.psum(mixed_part, 'vocab')  182 us
    psum x1, waiting for transfers between devices, body(): summed_grad = lax.psum(hidden_part, 'vocab')  178 us
    unnamed x9, waiting for transfers between devices  92.3 us
    psum x1, waiting for transfers between devices, body(): head_total = lax.psum(weight_acc.astype(jnp.bfloat16), 'dp')  74 us
    psum x1, blocking collectives, body(): lax.psum(jnp.sum(token_loss), ('dp', 'seq'))  60.4 us
    reduce_scatter x1, waiting for transfers between devices, body(): lax.psum_scatter(jnp.einsum('tbd,fd->tbf', row_block, out_proj, preferred...  43.5 us
    pmax x1, blocking collectives, body(): row_peak = lax.pmax(jnp.max(logits, axis=-1), 'vocab')  38.9 us
    psum x1, blocking collectives, body(): lax.psum((jnp.sum(jnp.exp(logits - row_peak[..., None]), axis=-1), local_...  32.1 us
  transfers between devices with their start and end apart: 7, of which 6 were waited for; matrix products, arithmetic and copies ran while one was open for 1% of the time, Pallas kernels for 0%

commit v1 on v0

--- a/solution.py
+++ b/solution.py
@@ -7,6 +7,11 @@
 HDIM = 256
 zloss_weight = 0.0001
 norm_epsilon = 1e-06
+
+
+def summed_here(x, name):
+    shards = lax.all_gather(x, name)
+    return jnp.sum(shards, axis=0)
 
 
 def body(
@@ -82,7 +87,7 @@
         "tbv,dv->tbd", grad_piece, head_weight, preferred_element_type=jnp.float32
     )
     head_total = lax.psum(weight_acc.astype(jnp.bfloat16), "dp")
-    summed_grad = lax.psum(hidden_part, "vocab")
+    summed_grad = summed_here(hidden_part, "vocab")
     gated = summed_grad * norm_gain
     dot_row = lax.psum(jnp.sum(gated * mixed_rows, axis=-1), "seq")
     mixed_grad = (

time: 882 us -> 837 us (0.949)
  waiting for transfers between devices: 583 us -> 535 us
    psum x1 -> x0, waiting for transfers between devices: 178 us -> none  [body(): summed_grad = lax.psum(hidden_part, 'vocab')]
    all_gather x0 -> x1, waiting for transfers between devices: none -> 140 us  [summed_here(): shards = lax.all_gather(x, name)]
    reduce_scatter x1, waiting for transfers between devices: 43.5 us -> 32.8 us  [body(): lax.psum_scatter(jnp.einsum('tbd,fd->tbf', row_block, out_proj, preferred...]
where the time goes in v1:
time: 837 us; the launch traced here: 836 us
  waiting for transfers between devices  535 us (64%)
  blocking collectives  240 us (29%)
  local copies, waits for them, and re-layouts  18.1 us (2%)
  between operations  17.5 us (2%)
  matrix products  13.7 us (2%)
  other arithmetic  11.6 us (1%)
    psum x1, waiting for transfers between devices, body(): lax.psum(mixed_part, 'vocab')  182 us
    all_gather x1, waiting for transfers between devices, summed_here(): shards = lax.all_gather(x, name)  140 us
    unnamed x9, waiting for transfers between devices  92.4 us
    psum x1, waiting for transfers between devices, body(): head_total = lax.psum(weight_acc.astype(jnp.bfloat16), 'dp')  73.7 us
    psum x1, blocking collectives, body(): lax.psum(jnp.sum(token_loss), ('dp', 'seq'))  60.4 us
    pmax x1, blocking collectives, body(): row_peak = lax.pmax(jnp.max(logits, axis=-1), 'vocab')  38.9 us
    reduce_scatter x1, waiting for transfers between devices, body(): lax.psum_scatter(jnp.einsum('tbd,fd->tbf', row_block, out_proj, preferred...  32.8 us
    psum x1, blocking collectives, body(): lax.psum((jnp.sum(jnp.exp(logits - row_peak[..., None]), axis=-1), local_...  32.1 us
  transfers between devices with their start and end apart: 7, of which 6 were waited for; matrix products, arithmetic and copies ran while one was open for 1% of the time, Pallas kernels for 0%

profile of v1, /device:TPU:1, one launch (start us, length us, event | category | flops | bytes accessed | tf_op | source)
XLA Modules:
  0.0 835.8 jit_solution(4153836605540388626)
XLA Ops:
  7.2 0.0 copy-start
  7.2 0.0 copy-start.7
  7.2 0.0 all-reduce.6.cloned.1.call-start
  8.1 21.9 %all_gather.19 = bf16[1,1024,256]{2,1,0:T(8,128)(2,1)S(1)} all-gather(bf16[1,128,256]{2,1,0:T(8,128)(2,1)} %param.11), channel_id=1, replica_groups=mesh['dp'=4,'seq'=8,'vocab'=16] {'seq'}, dimensions={1}, use_global_device_ids=true | all-gather | bytes 589824 | tf_op jit(solution)/shard_map/all_gather | solution.py:27
  30.0 20.0 %all_gather.18 = bf16[1,1024,256]{2,1,0:T(8,128)(2,1)S(1)} all-gather(bf16[1,128,256]{2,1,0:T(8,128)(2,1)} %param.10), channel_id=1, replica_groups=mesh['dp'=4,'seq'=8,'vocab'=16] {'seq'}, dimensions={1}, use_global_device_ids=true | all-gather | bytes 589824 | tf_op jit(solution)/shard_map/all_gather | solution.py:26
  50.1 1.1 fusion.43
  51.2 0.2 fusion.22
  51.4 0.2 fusion.3
  51.6 18.9 %all-gather = bf16[256,1,1,256]{3,0,2,1:T(8,128)(2,1)S(1)} all-gather(bf16[32,1,1,256]{3,0,2,1:T(8,128)(2,1)S(1)} %fusion.3), channel_id=2, replica_groups=mesh['dp'=4,'seq'=8,'vocab'=16] {'seq'}, dimensions={0}, use_global_device_ids=true | all-gather | bytes 147456 | tf_op jit(solution)/shard_map/all_gather | solution.py:47
  70.5 1.0 convolution_bitcast_fusion.1
  71.5 0.0 all-reduce.6.cloned.1.call-update
  71.6 0.0 all-reduce.10.cloned.1.call-start
  71.6 182.3 %all-reduce.6.cloned.1.call-done = f32[256,1,512]{2,0,1:T(8,128)} async-done(((f32[256,1,512]{2,0,1:T(8,128)}), f32[256,1,512]{2,0,1:T(8,128)}) %all-reduce.6.cloned.1.call-update) | async-done | bytes 524304 | tf_op jit(solution)/shard_map/psum | solution.py:51
  253.9 1.2 multiply_reduce_fusion.1
  255.1 13.7 %psum.50 = f32[256,1]{0,1:T(1,128)S(1)} all-reduce(f32[256,1]{0,1:T(1,128)S(1)} %bitcast.122), channel_id=1, replica_groups=mesh['dp'=4,'seq'=8,'vocab'=16] {'seq'}, use_global_device_ids=true, to_apply=%region_4.5 | all-reduce | flops 256 | bytes 2048 | tf_op jit(solution)/shard_map/psum | solution.py:52
  268.8 1.2 fusion.14
  270.0 0.7 copy-done.5
  270.7 2.0 convolution_bitcast_fusion
  272.7 6.1 copy.18
  278.8 0.0 all-reduce.10.cloned.1.call-update
  278.9 0.0 all-gather.4.cloned.1.call-start
  278.9 1.3 dynamic-slice
  280.9 92.3 %all-reduce.10.cloned.1.call-done = f32[256,1,2008]{2,1,0:T(1,128)} async-done(((f32[256,1,2008]{2,1,0:T(1,128)}), f32[256,1,2008]{2,1,0:T(1,128)}) %all-reduce.10.cloned.1.call-update) | async-done | bytes 2056208
  373.1 1.3 fusion.42
  374.5 38.9 %pmax.7 = f32[32,1]{0,1:T(1,128)S(1)} all-reduce(f32[32,1]{0,1:T(1,128)S(1)} %bitcast.129), channel_id=1, replica_groups=mesh['dp'=4,'seq'=8,'vocab'=16] {'vocab'}, use_global_device_ids=true, to_apply=%region_7.8 | all-reduce | flops 32 | bytes 256 | tf_op jit(solution)/shard_map/pmax | solution.py:68
  413.4 0.6 exponential_reduce_fusion
  413.9 0.2 fusion.11
  414.2 32.1 %all-reduce.1 = (f32[32,1]{0,1:T(1,128)S(1)}, f32[32,1]{0,1:T(1,128)S(1)}) all-reduce(f32[32,1]{0,1:T(1,128)S(1)} %bitcast.127, f32[32,1]{0,1:T(1,128)S(1)} %bitcast.128), channel_id=1, replica_groups=mesh['dp'=4,'seq'=8,'vocab'=16] {'vocab'}, use_global_device_ids=true, to_apply=%region_9.10 | all-reduce | flops 64 | bytes 512 | tf_op jit(solution)/shard_map/psum | solution.py:69
  446.3 0.6 fusion.38
  446.9 0.2 fusion.13
  447.0 20.6 %all_gather.21 = bf16[256,1,2008]{2,0,1:T(8,128)(2,1)S(1)} all-gather(bf16[32,1,2008]{2,0,1:T(8,128)(2,1)S(1)} %fusion.13), channel_id=1, replica_groups=mesh['dp'=4,'seq'=8,'vocab'=16] {'seq'}, dimensions={0}, use_global_device_ids=true | all-gather | bytes 1156608 | tf_op jit(solution)/shard_map/all_gather | solution.py:81
  467.6 1.0 copy-done.2
  468.6 1.5 fusion.4
  470.1 0.0 all-gather.4.cloned.1.call-update
  470.1 0.0 reduce-scatter.6.cloned.1.call-start
  470.2 140.3 %all-gather.4.cloned.1.call-done = f32[4096,512]{1,0:T(8,128)} async-done(((f32[256,512]{1,0:T(8,128)}), f32[4096,512]{1,0:T(8,128)}) %all-gather.4.cloned.1.call-update) | async-done | bytes 8388624 | tf_op jit(solution)/shard_map/all_gather | solution.py:13
  610.5 4.5 reduce.12
  614.9 0.2 multiply_reduce_fusion
  615.1 13.3 %psum.55 = f32[256,1]{0,1:T(1,128)S(1)} all-reduce(f32[256,1]{0,1:T(1,128)S(1)} %bitcast.123), channel_id=1, replica_groups=mesh['dp'=4,'seq'=8,'vocab'=16] {'seq'}, use_global_device_ids=true, to_apply=%region_17.18 | all-reduce | flops 256 | bytes 2048 | tf_op jit(solution)/shard_map/psum | solution.py:92
  628.4 2.0 convolution_bitcast_fusion.2
  630.3 0.0 reduce-scatter.6.cloned.1.call-update
  630.4 0.0 reduce-scatter.10.cloned.1.call-start
  630.4 32.8 %reduce-scatter.6.cloned.1.call-done = f32[32,1,256]{2,0,1:T(8,128)} async-done(((f32[256,1,256]{2,0,1:T(8,128)}), f32[32,1,256]{2,0,1:T(8,128)}) %reduce-scatter.6.cloned.1.call-update) | async-done | bytes 32784 | tf_op jit(solution)/shard_map/reduce_scatter | solution.py:97
  663.2 1.2 fusion.1
  664.4 0.0 copy-start.9
  664.4 2.0 copy.22
  666.4 2.2 copy.28
  668.6 0.0 reduce-scatter.10.cloned.1.call-update
  668.7 0.0 reduce-scatter.8.cloned.1.call-start
  668.7 1.4 multiply_reduce_fusion.2
  670.2 1.2 fusion
  671.4 0.0 reduce-scatter.8.cloned.1.call-update
  671.4 0.0 all-reduce.8.cloned.1.call-start
  671.5 2.0 convolution_convert_fusion
  673.5 0.0 all-reduce.8.cloned.1.call-update
  673.5 60.4 %psum.53 = f32[]{:T(128)} all-reduce(f32[]{:T(128)} %get-tuple-element.26), channel_id=1, replica_groups=mesh['dp'=4,'seq'=8,'vocab'=16] {'dp','seq'}, use_global_device_ids=true, to_apply=%region_13.14 | all-reduce | flops 1 | bytes 8 | tf_op jit(solution)/shard_map/psum | solution.py:74
  734.6 0.0 reduce-scatter.10.cloned.1.call-done
  734.6 0.9 reshape_bitcast_fusion
  735.5 0.1 copy.23
  735.7 0.8 copy.21
  736.5 13.2 %reduce-scatter.8.cloned.1.call-done = bf16[1,128,256]{2,1,0:T(8,128)(2,1)} async-done(((bf16[1,1024,256]{2,1,0:T(8,128)(2,1)}), bf16[1,128,256]{2,1,0:T(8,128)(2,1)}) %reduce-scatter.8.cloned.1.call-update) | async-done | bytes 65552 | tf_op jit(solution)/shard_map/reduce_scatter | solution.py:118
  749.7 1.5 convert_element_type.128
  751.2 73.7 %all-reduce.8.cloned.1.call-done = bf16[512,2008]{0,1:T(8,128)(2,1)} async-done(((bf16[512,2008]{0,1:T(8,128)(2,1)}), bf16[512,2008]{0,1:T(8,128)(2,1)}) %all-reduce.8.cloned.1.call-update) | async-done | bytes 2056208 | tf_op jit(solution)/shard_map/psum | solution.py:89
  824.8 3.0 copy.33
  (25 shorter events, 0.1 us)
Async XLA Ops:
  7.2 263.5 %copy-start = (bf16[512,2008]{0,1:T(8,128)(2,1)S(1)}, bf16[512,2008]{0,1:T(8,128)(2,1)}, u32[]{:S(2)}) copy-start(bf16[512,2008]{0,1:T(8,128)(2,1)} %param.16) | copy-start | bytes 6168580
  7.2 63.3 %copy-start.7 = (bf16[256,512]{1,0:T(8,128)(2,1)S(1)}, bf16[256,512]{1,0:T(8,128)(2,1)}, u32[]{:S(2)}) copy-start(bf16[256,512]{1,0:T(8,128)(2,1)} %param.13) | copy-start | bytes 786436
  7.2 246.7 %all-reduce.6.cloned.1.call-start = ((), (), s32[]{:S(2)}) async-start(), calls=%async_computation.3 | async-start | bytes 1048576 | tf_op jit(solution)/shard_map/psum | solution.py:51
  30.0 21.4 %copy-start.8 = (bf16[1,1024,256]{2,1,0:T(8,128)(2,1)}, bf16[1,1024,256]{2,1,0:T(8,128)(2,1)S(1)}, u32[]{:S(2)}) copy-start(bf16[1,1024,256]{2,1,0:T(8,128)(2,1)S(1)} %all_gather.19) | copy-start | bytes 1572868
  30.0 223.9 %copy-start.4 = (bf16[1,256,512]{2,1,0:T(8,128)(2,1)S(1)}, bf16[1,256,512]{2,1,0:T(8,128)(2,1)}, u32[]{:S(2)}) copy-start(bf16[1,256,512]{2,1,0:T(8,128)(2,1)} %param.14) | copy-start | bytes 786436
  50.1 218.8 %copy-start.11 = (f32[512]{0:T(512)S(1)}, f32[512]{0:T(512)}, u32[]{:S(2)}) copy-start(f32[512]{0:T(512)} %param.15) | copy-start | bytes 6148
  71.6 301.5 %all-reduce.10.cloned.1.call-start = ((), (), s32[]{:S(2)}) async-start(), calls=%async_computation.9 | async-start | bytes 4194304
  270.0 0.7 copy-start.5
  278.8 135.1 %copy-start.12 = (s32[1,32]{1,0:T(1,128)S(1)}, s32[1,32]{1,0:T(1,128)}, u32[]{:S(2)}) copy-start(s32[1,32]{1,0:T(1,128)} %param.17) | copy-start | bytes 388
  278.9 331.6 %all-gather.4.cloned.1.call-start = ((), (), s32[]{:S(2)}) async-start(), calls=%async_computation.7 | async-start | bytes 8912896 | tf_op jit(solution)/shard_map/all_gather | solution.py:13
  467.6 1.0 copy-start.2
  470.1 193.1 %reduce-scatter.6.cloned.1.call-start = ((), (), s32[]{:S(2)}) async-start(), calls=%async_computation.5 | async-start | bytes 294912 | tf_op jit(solution)/shard_map/reduce_scatter | solution.py:97
  610.5 4.5 copy-start.1
  630.4 104.2 %reduce-scatter.10.cloned.1.call-start = ((), (), s32[]{:S(2)}) async-start(), calls=%async_computation.8 | async-start | bytes 589824
  663.2 5.5 copy-start.10
  664.4 5.7 copy-start.9
  666.4 5.0 copy-start.3
  666.4 5.0 copy-start.6
  668.7 81.0 %reduce-scatter.8.cloned.1.call-start = ((), (), s32[]{:S(2)}) async-start(), calls=%async_computation.6 | async-start | bytes 589824 | tf_op jit(solution)/shard_map/reduce_scatter | solution.py:118
  671.4 153.4 %all-reduce.8.cloned.1.call-start = ((), (), s32[]{:S(2)}) async-start(), calls=%async_computation.4 | async-start | bytes 4112384 | tf_op jit(solution)/shard_map/psum | solution.py:89
Sparse Core Ops, SparseCore 0:
  71.7 182.1 all-reduce.5
  279.0 94.0 all-reduce.9
  470.3 140.1 all-gather.3
  630.5 32.7 reduce-scatter.5
  668.8 39.3 reduce-scatter.9
  711.1 38.5 reduce-scatter.7
  753.2 71.5 all-reduce.7
